TPU v7x, 128 devices: a whole 4x4x4 slice. The times are simulated.
128 devices in a mesh: ctx: 16 (over z, y), ch: 8 (over x, core).
Axes of the slice: x: 4, y: 4, z: 4, core: 2. Of those that a mesh axis runs over, the one named last changes fastest.
Arguments:
- outer_gate: bfloat16 [4096, 4096], P('ctx', 'ch'), may hold values from -6 to 6
- inner_gate: bfloat16 [4096, 4096], P('ctx', 'ch'), may hold values from -6 to 6
- values_in: bfloat16 [4096, 4096], P('ctx', 'ch'), may hold values from -6 to 6
- filters: float32 [4096, 4096], P('ctx', 'ch'), as said below
- skip_gain: float32 [4096], P('ch'), may hold values from 0.5 to 1.5
- w_out: bfloat16 [4096, 4096], P('ch', 'ctx'), may hold values from -0.125 to 0.125
Outputs:
- mixed: bfloat16 [4096, 4096], P('ctx', 'ch')
Inputs may be any that keep to these rules, and one draw needn't show every extreme that they name: `filters`: finite values.
All inputs are finite; a program needn't handle non-finite values.
Results may differ from a plain program's by a relative error of at most 0.022.
Values may be sent and summed in bfloat16 or wider, within the bound.
A program may use at most 64 MiB of HBM per device.

v0:
```python
import math
import jax
import jax.numpy as jnp
from jax import lax
from jax.sharding import PartitionSpec as P


def from_behind(block, axis, distance):
    devices = range(lax.axis_size(axis))
    route = [(i - distance, i) for i in devices if i - distance in devices]
    return lax.ppermute(block, axis, route)


def forward_table(block):
    length = 2 * block
    rows = jnp.arange(block, dtype=jnp.int32)[:, None]
    freqs = jnp.arange(length, dtype=jnp.int32)[None, :]
    angles = 2.0 * math.pi / length * (rows * freqs % length).astype(jnp.float32)
    return jnp.concatenate([jnp.cos(angles), -jnp.sin(angles)], axis=1)


def inverse_table(block):
    length = 2 * block
    freqs = jnp.arange(length, dtype=jnp.int32)[:, None]
    places = jnp.arange(length, dtype=jnp.int32)[None, :]
    angles = 2.0 * math.pi / length * (freqs * places % length).astype(jnp.float32)
    return jnp.concatenate([jnp.cos(angles), -jnp.sin(angles)], axis=0) / length


def split_table(table):
    upper_part = table.astype(jnp.bfloat16)
    lower_part = (table - upper_part.astype(jnp.float32)).astype(jnp.bfloat16)
    return (upper_part, lower_part)


def spectrum(series, table):
    return lax.dot_general(
        series,
        table,
        (((0,), (0,)), ((), ())),
        precision=lax.Precision.HIGH,
        preferred_element_type=jnp.float32,
    )


def narrow_spectrum(series, tables):
    dims = (((0,), (0,)), ((), ()))
    first = lax.dot_general(series, tables[0], dims, preferred_element_type=jnp.float32)
    return first + lax.dot_general(series, tables[1], dims, preferred_element_type=jnp.float32)


def complex_product(left, right):
    half = left.shape[-1] // 2
    left_re, left_im = (left[..., :half], left[..., half:])
    right_re, right_im = (right[..., :half], right[..., half:])
    return jnp.concatenate(
        [left_re * right_re - left_im * right_im, left_re * right_im + left_im * right_re], axis=-1
    )


def per_device(outer_gate, inner_gate, values_in, filters, skip_gain, w_out):
    block = outer_gate.shape[0]
    chans = outer_gate.shape[1]
    length = 2 * block
    gated = (inner_gate.astype(jnp.float32) * values_in.astype(jnp.float32)).astype(jnp.bfloat16)
    forward = forward_table(block)
    forward_parts = split_table(forward)
    inverse = inverse_table(block)
    whole_filter = lax.all_gather(filters.astype(jnp.bfloat16), "ctx", axis=0, tiled=True).astype(
        filters.dtype
    )
    mine = lax.axis_index("ctx")
    empty = jnp.zeros((chans, 2 * length), jnp.float32)
    piece = lax.all_gather(gated[None], "ctx", axis=0, tiled=True)

    def one_block(k, acc):
        distance = mine - k

        def live(inner):
            lag_rows = lax.dynamic_slice_in_dim(
                whole_filter, jnp.maximum(distance, 0) * block, block, 0
            )
            source = lax.dynamic_index_in_dim(piece, k, 0, keepdims=False)
            return inner + complex_product(
                narrow_spectrum(source, forward_parts), spectrum(lag_rows, forward)
            )

        return lax.cond(distance >= 0, live, lambda inner: inner, acc)

    summed = lax.fori_loop(0, piece.shape[0], one_block, empty)
    wave = lax.dot_general(
        inverse,
        summed,
        (((0,), (1,)), ((), ())),
        precision=lax.Precision.HIGH,
        preferred_element_type=jnp.float32,
    )
    carried = from_behind(wave[block:].astype(jnp.bfloat16), "ctx", 1).astype(jnp.float32)
    conv = wave[:block] + carried
    mix_in = (
        outer_gate.astype(jnp.float32) * (conv + skip_gain[None, :] * gated.astype(jnp.float32))
    ).astype(jnp.bfloat16)
    partial_rows = jnp.dot(
        mix_in, lax.all_gather(w_out, "ctx", axis=1, tiled=True), preferred_element_type=jnp.float32
    )
    return lax.psum_scatter(
        partial_rows.astype(jnp.bfloat16), "ch", scatter_dimension=1, tiled=True
    )


def solution(mesh):
    placed = (
        P("ctx", "ch"),
        P("ctx", "ch"),
        P("ctx", "ch"),
        P("ctx", "ch"),
        P("ch"),
        P("ch", "ctx"),
    )
    return jax.shard_map(
        per_device, mesh=mesh, in_specs=placed, out_specs=P("ctx", "ch"), check_vma=False
    )
```

profile of v0, /device:TPU:0, one launch (start us, length us, event | category | flops | bytes accessed | tf_op | source)
XLA Modules:
  0.0 322.4 jit_solution(1819847222807152443)
XLA Ops:
  6.5 0.0 all-gather.5.cloned.1.call-start
  6.5 1.8 convert_element_type.66
  8.3 0.0 all-gather.5.cloned.1.call-update
  8.3 0.0 all-gather.9.cloned.1.call-start
  8.4 1.8 multiply_convert_fusion
  10.2 0.0 all-gather.9.cloned.1.call-update
  10.2 0.0 all-gather.7.cloned.1.call-start
  10.3 0.7 all-gather.7.cloned.1.call-update
  10.9 0.0 reduce-scatter.2.cloned.1.call-start
  11.0 2.1 sine_negate_fusion.1
  13.1 0.9 fusion.35
  13.9 1.0 pad_maximum_fusion
  14.9 5.0 %sine_negate_fusion = (f32[512,512]{1,0:T(8,128)}, f32[512,512]{1,0:T(8,128)}) fusion(), kind=kLoop, calls=%fused_computation.28 | loop fusion | flops 3932160 | bytes 2097152 | tf_op jit(solution)/shard_map/neg | solution.py:27
  19.9 43.8 %all-gather.5.cloned.1.call-done = bf16[4096,512]{1,0:T(8,128)(2,1)} async-done(((bf16[256,512]{1,0:T(8,128)(2,1)}), bf16[4096,512]{1,0:T(8,128)(2,1)}) %all-gather.5.cloned.1.call-update) | async-done | bytes 4194320 | tf_op jit(solution)/shard_map/all_gather | solution.py:69
  63.7 6.6 %convert_element_type.67 = f32[4096,512]{1,0:T(8,128)} convert(bf16[4096,512]{1,0:T(8,128)(2,1)} %all-gather.5.cloned.1.call-done) | non-fusion elementwise | flops 2097152 | bytes 12582912 | tf_op jit(solution)/shard_map/convert_element_type | solution.py:69
  70.3 46.8 %all-gather.9.cloned.1.call-done = bf16[4096,512]{1,0:T(8,128)(2,1)} async-done(((bf16[256,512]{1,0:T(8,128)(2,1)}), bf16[4096,512]{1,0:T(8,128)(2,1)}) %all-gather.9.cloned.1.call-update) | async-done | bytes 4194320 | tf_op jit(solution)/shard_map/all_gather | solution.py:74
  117.1 1.6 broadcast_in_dim.4
  118.7 9.3 %while.16 = (s32[]{:T(128)}, f32[512,1024]{1,0:T(8,128)}, s32[]{:T(128)}, bf16[16,256,512]{2,1,0:T(8,128)(2,1)}, bf16[256,1024]{1,0:T(8,128)(2,1)}, /*index=5*/b...) while((s32[]{:T(128)}, f32[512,1024]{1,0:T(8,128)}, ...), condition=%wide.region_3.4_spmd, body=%wide.region_0.3_spmd.sunk | while | flops 1345323008 | bytes 26214732 | solution.py:90
  118.7 9.0 %conditional.2 = (f32[512,1024]{1,0:T(8,128)}) conditional(s32[]{:T(128)} %convert_element_type.104, f32[512,1024]{1,0:T(8,128)} %get-tuple-element.261, (s32[]{:T(128)}, bf16[16,256,512]{2,1,0:T(8,128)(2,1)}, bf16[256,1024]{1,0:T(8,128)(2,1)}, bf16[256,1024]{1,0:T(8,128)(2,1)}, s32[]{:T(128)}, /*index=5*/f32[4096,512]{1,0:T(8,128)}, ...), branch_computations={%region_1.1_spmd, %region_2.2_spmd} | conditional | flops 1345323008 | bytes 26214540 | solution.py:88
  118.7 0.0 copy-start
  118.7 1.6 fusion.3
  120.3 0.0 copy-done
  120.3 1.4 convolution_add_fusion
  121.7 2.1 fusion
  123.8 0.5 multiply_subtract_fusion
  124.3 3.3 %maximum_add_fusion = f32[512,1024]{1,0:T(8,128)} fusion(f32[512,1024]{1,0:T(8,128)} %get-tuple-element.158, f32[512,512]{1,0:T(8,128)S(1)} %get-tuple-element.194, f32[512,512]{1,0:T(8,128)S(1)} %get-tuple-element.193), kind=kLoop, calls=%fused_computation | loop fusion | flops 1048576 | bytes 6291456 | tf_op jit(solution)/shard_map/while/body/eval_jaxpr/cond/branch_1_fun/add | solution.py:84
  128.0 0.0 copy-start.1
  128.0 0.0 copy-start.2
  128.0 0.0 copy-start.3
  128.0 5.9 %fusion.10 = f32[512,512]{1,0:T(8,128)S(1)} fusion(f32[512,1024]{1,0:T(8,128)} %get-tuple-element.176, f32[512,512]{1,0:T(8,128)} %get-tuple-element.199, f32[512,512]{1,0:T(8,128)} %get-tuple-element.200), kind=kOutput, calls=%fused_computation.16 | convolution fusion | flops 1611661312 | bytes 5242880 | tf_op jit(solution)/shard_map/dot_general | solution.py:91
  134.0 12.3 %collective-permute-start = (bf16[256,512]{1,0:T(8,128)(2,1)S(1)}, bf16[256,512]{1,0:T(8,128)(2,1)S(1)}, u32[]{:S(2)}, u32[]{:S(2)}) collective-permute-start(bf16[256,512]{1,0:T(8,128)(2,1)S(1)} %slice.44), channel_id=1, source_target_pairs={{0,8},{8,16},{16,24},{24,32},{32,40},{40,48},{48,56},{56,64},{64,7... | collective-permute-start | bytes 786440 | tf_op jit(solution)/shard_map/ppermute | solution.py:11
  146.3 32.7 %all-gather.7.cloned.1.call-done = bf16[512,4096]{1,0:T(8,128)(2,1)} async-done(((bf16[512,256]{1,0:T(8,128)(2,1)}), bf16[512,4096]{1,0:T(8,128)(2,1)}) %all-gather.7.cloned.1.call-update) | async-done | bytes 4194320 | tf_op jit(solution)/shard_map/all_gather | solution.py:104
  179.0 0.0 collective-permute-done
  179.0 0.0 copy-done.1
  179.0 0.0 copy-done.2
  179.0 0.0 copy-done.3
  179.0 4.8 %convolution_convert_fusion = bf16[256,4096]{1,0:T(8,128)(2,1)} fusion(bf16[512,4096]{1,0:T(8,128)(2,1)} %all-gather.7.cloned.1.call-done, f32[512,512]{1,0:T(8,128)S(1)} %fusion.10, bf16[256,512]{1,0:T(8,128)(2,1)S(1)} %copy-done.1, bf16[256,512]{1,0:T(8,128)(2,1)S(1)} %collective-permute-done, bf16[256,512]{1,0:T(8,128)(2,1)S(1)} %copy-done.2, ...), kind=kOutput, calls=%fused_computation.14 | convolution fusion | flops 1075838976 | bytes 7604224 | tf_op jit(solution)/shard_map/dot_general | solution.py:103
  183.8 0.0 reduce-scatter.2.cloned.1.call-update
  183.8 132.1 %reduce-scatter.2.cloned.1.call-done = bf16[256,512]{1,0:T(8,128)(2,1)} async-done(((bf16[256,4096]{1,0:T(8,128)(2,1)}), bf16[256,512]{1,0:T(8,128)(2,1)}) %reduce-scatter.2.cloned.1.call-update) | async-done | bytes 262160 | tf_op jit(solution)/shard_map/reduce_scatter | solution.py:106
  (16 shorter events, 0.1 us)
Async XLA Ops:
  6.5 57.1 %all-gather.5.cloned.1.call-start = ((), (), s32[]{:S(2)}) async-start(), calls=%async_computation.1 | async-start | bytes 4456448 | tf_op jit(solution)/shard_map/all_gather | solution.py:69
  8.3 108.7 %all-gather.9.cloned.1.call-start = ((), (), s32[]{:S(2)}) async-start(), calls=%async_computation.4 | async-start | bytes 4456448 | tf_op jit(solution)/shard_map/all_gather | solution.py:74
  10.2 168.8 %all-gather.7.cloned.1.call-start = ((), (), s32[]{:S(2)}) async-start(), calls=%async_computation.2 | async-start | bytes 4456448 | tf_op jit(solution)/shard_map/all_gather | solution.py:104
  10.9 304.9 %reduce-scatter.2.cloned.1.call-start = ((), (), s32[]{:S(2)}) async-start(), calls=%async_computation.3 | async-start | bytes 2359296 | tf_op jit(solution)/shard_map/reduce_scatter | solution.py:106
  118.7 1.6 copy-start
  128.0 51.0 %copy-start.1 = (bf16[256,512]{1,0:T(8,128)(2,1)S(1)}, bf16[256,512]{1,0:T(8,128)(2,1)}, u32[]{:S(2)}) copy-start(bf16[256,512]{1,0:T(8,128)(2,1)} %multiply_convert_fusion) | copy-start | bytes 786436
  128.0 51.0 %copy-start.2 = (bf16[256,512]{1,0:T(8,128)(2,1)S(1)}, bf16[256,512]{1,0:T(8,128)(2,1)}, u32[]{:S(2)}) copy-start(bf16[256,512]{1,0:T(8,128)(2,1)} %param.10) | copy-start | bytes 786436
  128.0 51.0 %copy-start.3 = (f32[512]{0:T(512)S(1)}, f32[512]{0:T(512)}, u32[]{:S(2)}) copy-start(f32[512]{0:T(512)} %param.14) | copy-start | bytes 6148
  134.0 45.0 %collective-permute-start = (bf16[256,512]{1,0:T(8,128)(2,1)S(1)}, bf16[256,512]{1,0:T(8,128)(2,1)S(1)}, u32[]{:S(2)}, u32[]{:S(2)}) collective-permute-start(bf16[256,512]{1,0:T(8,128)(2,1)S(1)} %slice.44), channel_id=1, source_target_pairs={{0,8},{8,16},{16,24},{24,32},{32,40},{40,48},{48,56},{56,64},{64,7... | collective-permute-start | bytes 786440 | tf_op jit(solution)/shard_map/ppermute | solution.py:11
Sparse Core Ops, SparseCore 0:
  9.5 54.1 all-gather.4
  65.8 51.2 all-gather.8
  119.2 59.7 all-gather.6
  183.9 131.8 reduce-scatter.1
where the time goes:
time: 325 us; the launch traced here: 322 us
  waiting for transfers between devices  256 us (79%)
  other arithmetic  22.9 us (7%)
  matrix products  15.8 us (5%)
  between operations  13.2 us (4%)
  starting transfers between devices  12.5 us (4%)
    reduce_scatter x1, waiting for transfers between devices, per_device(): lax.psum_scatter(partial_rows.astype(jnp.bfloat16), 'ch', scatter_dimensi...  132 us
    all_gather x1, waiting for transfers between devices, per_device(): piece = lax.all_gather(gated[None], 'ctx', axis=0, tiled=True)  46.8 us
    all_gather x1, waiting for transfers between devices, per_device(): lax.all_gather(filters.astype(jnp.bfloat16), 'ctx', axis=0, tiled=True)  43.8 us
    all_gather x1, waiting for transfers between devices, per_device(): lax.all_gather(w_out, 'ctx', axis=1, tiled=True)  32.7 us
    ppermute x1, starting transfers between devices, from_behind(): return lax.ppermute(block, axis, route)  12.3 us
    convert_element_type x1, other arithmetic, per_device(): lax.all_gather(filters.astype(jnp.bfloat16), 'ctx', axis=0, tiled=True)  6.63 us
  transfers between devices with their start and end apart: 5, of which 4 were waited for; matrix products, arithmetic and copies ran while one was open for 10% of the time, Pallas kernels for 0%

commit v1 on v0

--- a/solution.py
+++ b/solution.py
@@ -3,6 +3,19 @@
 import jax.numpy as jnp
 from jax import lax
 from jax.sharding import PartitionSpec as P
+
+
+def gather_around(array, axis, dim):
+    ways = lax.axis_size(axis)
+    up = [(d, (d + 1) % ways) for d in range(ways)]
+    down = [(d, (d - 1) % ways) for d in range(ways)]
+    earlier, later = ([array], [array])
+    for _ in range(ways // 2):
+        earlier.append(lax.ppermute(earlier[-1], axis, up))
+    for _ in range((ways - 1) // 2):
+        later.append(lax.ppermute(later[-1], axis, down))
+    line = jnp.concatenate([*earlier[::-1], *later[1:]], axis=dim)
+    return jnp.roll(line, (lax.axis_index(axis) - ways // 2) * array.shape[dim], axis=dim)
 
 
 def from_behind(block, axis, distance):
@@ -101,7 +114,7 @@
         outer_gate.astype(jnp.float32) * (conv + skip_gain[None, :] * gated.astype(jnp.float32))
     ).astype(jnp.bfloat16)
     partial_rows = jnp.dot(
-        mix_in, lax.all_gather(w_out, "ctx", axis=1, tiled=True), preferred_element_type=jnp.float32
+        mix_in, gather_around(w_out, "ctx", 1), preferred_element_type=jnp.float32
     )
     return lax.psum_scatter(
         partial_rows.astype(jnp.bfloat16), "ch", scatter_dimension=1, tiled=True

time: 325 us -> 307 us (0.945)
  waiting for transfers between devices: 256 us -> 181 us
  starting transfers between devices: 12.5 us -> 45.4 us
  local copies, waits for them, and re-layouts: 1.64 us -> 29.8 us
    ppermute x0 -> x15, waiting for transfers between devices: none -> 55.3 us  [the longest x8 49.8 us: gather_around(): earlier.append(lax.ppermute(earlier[-1], axis, up))]
    all_gather x1, waiting for transfers between devices: 46.8 us -> 0.01 us  [per_device(): piece = lax.all_gather(gated[None], 'ctx', axis=0, tiled=True)]
    all_gather x1, waiting for transfers between devices: 43.8 us -> 0.01 us  [per_device(): lax.all_gather(filters.astype(jnp.bfloat16), 'ctx', axis=0, tiled=True)]
    ppermute x0 -> x15, starting transfers between devices: none -> 40.3 us  [the longest x7 38.6 us: gather_around(): later.append(lax.ppermute(later[-1], axis, down))]
    all_gather x1 -> x0, waiting for transfers between devices: 32.7 us -> none  [per_device(): lax.all_gather(w_out, 'ctx', axis=1, tiled=True)]
    unnamed x6 -> x47, local copies, waits for them, and re-layouts: 0.02 us -> 27.9 us
    ppermute x1, starting transfers between devices: 12.3 us -> 4.96 us  [from_behind(): return lax.ppermute(block, axis, route)]
    reduce_scatter x1, waiting for transfers between devices: 132 us -> 125 us  [per_device(): lax.psum_scatter(partial_rows.astype(jnp.bfloat16), 'ch', scatter_dimensi...]
  transfers between devices with their start and end apart: 5 -> 19, of which waited for: 4 -> 10; matrix products, arithmetic and copies ran while one was open for 10% -> 15% of each run, Pallas kernels for 0% -> 0%
where the time goes in v1:
time: 307 us; the launch traced here: 305 us
  waiting for transfers between devices  181 us (59%)
  starting transfers between devices  45.4 us (15%)
  local copies, waits for them, and re-layouts  29.8 us (10%)
  other arithmetic  20.2 us (7%)
  matrix products  15.2 us (5%)
  between operations  13.2 us (4%)
    reduce_scatter x1, waiting for transfers between devices, per_device(): lax.psum_scatter(partial_rows.astype(jnp.bfloat16), 'ch', scatter_dimensi...  125 us
    ppermute x8, waiting for transfers between devices, gather_around(): earlier.append(lax.ppermute(earlier[-1], axis, up))  49.8 us
    ppermute x7, starting transfers between devices, gather_around(): later.append(lax.ppermute(later[-1], axis, down))  38.6 us
    unnamed x47, local copies, waits for them, and re-layouts  27.9 us
    convert_element_type x1, other arithmetic, per_device(): lax.all_gather(filters.astype(jnp.bfloat16), 'ctx', axis=0, tiled=True)  6.66 us
  transfers between devices with their start and end apart: 19, of which 10 were waited for; matrix products, arithmetic and copies ran while one was open for 15% of the time, Pallas kernels for 0%

profile of v1, /device:TPU:0, one launch (start us, length us, event | category | flops | bytes accessed | tf_op | source)
XLA Modules:
  0.0 305.2 jit_solution(7096015996779961958)
XLA Ops:
  6.5 1.8 convert_element_type.66
  8.4 1.8 multiply_convert_fusion
  10.3 1.7 collective-permute-start.1
  12.0 11.4 %collective-permute-done.1 = bf16[512,256]{1,0:T(8,128)(2,1)S(1)} collective-permute-done((bf16[512,256]{1,0:T(8,128)(2,1)}, bf16[512,256]{1,0:T(8,128)(2,1)S(1)}, u32[]{:S(2)}, u32[]{:S(2)}) %collective-permute-start.1) | collective-permute-done | bytes 262176 | tf_op jit(solution)/shard_map/ppermute | solution.py:14
  23.4 5.3 %collective-permute-start.9 = (bf16[512,256]{1,0:T(8,128)(2,1)}, bf16[512,256]{1,0:T(8,128)(2,1)S(1)}, u32[]{:S(2)}, u32[]{:S(2)}) collective-permute-start(bf16[512,256]{1,0:T(8,128)(2,1)} %param.15), channel_id=1, source_target_pairs={{0,120},{8,0},{16,8},{24,16},{32,24},{40,32},{48,40},{56,48},{64,5... | collective-permute-start | bytes 786440 | tf_op jit(solution)/shard_map/ppermute | solution.py:16
  28.8 9.2 %collective-permute-done.2 = bf16[512,256]{1,0:T(8,128)(2,1)S(1)} collective-permute-done((bf16[512,256]{1,0:T(8,128)(2,1)S(1)}, bf16[512,256]{1,0:T(8,128)(2,1)S(1)}, u32[]{:S(2)}, u32[]{:S(2)}) %collective-permute-start.2) | collective-permute-done | bytes 262176 | tf_op jit(solution)/shard_map/ppermute | solution.py:14
  38.0 5.3 %collective-permute-start.10 = (bf16[512,256]{1,0:T(8,128)(2,1)S(1)}, bf16[512,256]{1,0:T(8,128)(2,1)S(1)}, u32[]{:S(2)}, u32[]{:S(2)}) collective-permute-start(bf16[512,256]{1,0:T(8,128)(2,1)S(1)} %collective-permute-done.9), channel_id=1, source_target_pairs={{0,120},{8,0},{16,8},{24,16},{32,24},{40,32},{48,40},{56,48},{64,5... | collective-permute-start | bytes 786440 | tf_op jit(solution)/shard_map/ppermute | solution.py:16
  43.4 5.4 %collective-permute-done.3 = bf16[512,256]{1,0:T(8,128)(2,1)S(1)} collective-permute-done((bf16[512,256]{1,0:T(8,128)(2,1)S(1)}, bf16[512,256]{1,0:T(8,128)(2,1)S(1)}, u32[]{:S(2)}, u32[]{:S(2)}) %collective-permute-start.3) | collective-permute-done | bytes 262176 | tf_op jit(solution)/shard_map/ppermute | solution.py:14
  48.7 3.3 %collective-permute-done.10 = bf16[512,256]{1,0:T(8,128)(2,1)S(1)} collective-permute-done((bf16[512,256]{1,0:T(8,128)(2,1)S(1)}, bf16[512,256]{1,0:T(8,128)(2,1)S(1)}, u32[]{:S(2)}, u32[]{:S(2)}) %collective-permute-start.10) | collective-permute-done | bytes 262176 | tf_op jit(solution)/shard_map/ppermute | solution.py:16
  52.1 5.8 %collective-permute-start.11 = (bf16[512,256]{1,0:T(8,128)(2,1)S(1)}, bf16[512,256]{1,0:T(8,128)(2,1)S(1)}, u32[]{:S(2)}, u32[]{:S(2)}) collective-permute-start(bf16[512,256]{1,0:T(8,128)(2,1)S(1)} %collective-permute-done.10), channel_id=1, source_target_pairs={{0,120},{8,0},{16,8},{24,16},{32,24},{40,32},{48,40},{56,48},{64,5... | collective-permute-start | bytes 786440 | tf_op jit(solution)/shard_map/ppermute | solution.py:16
  57.9 8.0 %collective-permute-done.4 = bf16[512,256]{1,0:T(8,128)(2,1)S(1)} collective-permute-done((bf16[512,256]{1,0:T(8,128)(2,1)S(1)}, bf16[512,256]{1,0:T(8,128)(2,1)S(1)}, u32[]{:S(2)}, u32[]{:S(2)}) %collective-permute-start.4) | collective-permute-done | bytes 262176 | tf_op jit(solution)/shard_map/ppermute | solution.py:14
  65.9 2.1 collective-permute-done.11
  67.9 5.8 %collective-permute-start.12 = (bf16[512,256]{1,0:T(8,128)(2,1)S(1)}, bf16[512,256]{1,0:T(8,128)(2,1)S(1)}, u32[]{:S(2)}, u32[]{:S(2)}) collective-permute-start(bf16[512,256]{1,0:T(8,128)(2,1)S(1)} %collective-permute-done.11), channel_id=1, source_target_pairs={{0,120},{8,0},{16,8},{24,16},{32,24},{40,32},{48,40},{56,48},{64,5... | collective-permute-start | bytes 786440 | tf_op jit(solution)/shard_map/ppermute | solution.py:16
  73.7 6.1 %collective-permute-done.5 = bf16[512,256]{1,0:T(8,128)(2,1)S(1)} collective-permute-done((bf16[512,256]{1,0:T(8,128)(2,1)S(1)}, bf16[512,256]{1,0:T(8,128)(2,1)S(1)}, u32[]{:S(2)}, u32[]{:S(2)}) %collective-permute-start.5) | collective-permute-done | bytes 262176 | tf_op jit(solution)/shard_map/ppermute | solution.py:14
  79.8 5.3 %collective-permute-start.13 = (bf16[512,256]{1,0:T(8,128)(2,1)S(1)}, bf16[512,256]{1,0:T(8,128)(2,1)S(1)}, u32[]{:S(2)}, u32[]{:S(2)}) collective-permute-start(bf16[512,256]{1,0:T(8,128)(2,1)S(1)} %collective-permute-done.12), channel_id=1, source_target_pairs={{0,120},{8,0},{16,8},{24,16},{32,24},{40,32},{48,40},{56,48},{64,5... | collective-permute-start | bytes 786440 | tf_op jit(solution)/shard_map/ppermute | solution.py:16
  85.1 5.1 %collective-permute-done.6 = bf16[512,256]{1,0:T(8,128)(2,1)} collective-permute-done((bf16[512,256]{1,0:T(8,128)(2,1)S(1)}, bf16[512,256]{1,0:T(8,128)(2,1)}, u32[]{:S(2)}, u32[]{:S(2)}) %collective-permute-start.6) | collective-permute-done | bytes 262176 | tf_op jit(solution)/shard_map/ppermute | solution.py:14
  90.3 2.1 sine_negate_fusion.1
  92.4 1.0 pad_maximum_fusion
  93.3 5.3 %collective-permute-start.14 = (bf16[512,256]{1,0:T(8,128)(2,1)S(1)}, bf16[512,256]{1,0:T(8,128)(2,1)S(1)}, u32[]{:S(2)}, u32[]{:S(2)}) collective-permute-start(bf16[512,256]{1,0:T(8,128)(2,1)S(1)} %collective-permute-done.13), channel_id=1, source_target_pairs={{0,120},{8,0},{16,8},{24,16},{32,24},{40,32},{48,40},{56,48},{64,5... | collective-permute-start | bytes 786440 | tf_op jit(solution)/shard_map/ppermute | solution.py:16
  98.7 4.7 %collective-permute-done.7 = bf16[512,256]{1,0:T(8,128)(2,1)S(1)} collective-permute-done((bf16[512,256]{1,0:T(8,128)(2,1)}, bf16[512,256]{1,0:T(8,128)(2,1)S(1)}, u32[]{:S(2)}, u32[]{:S(2)}) %collective-permute-start.7) | collective-permute-done | bytes 262176 | tf_op jit(solution)/shard_map/ppermute | solution.py:14
  103.3 0.8 fusion.37
  104.2 5.0 %sine_negate_fusion = (f32[512,512]{1,0:T(8,128)}, f32[512,512]{1,0:T(8,128)}) fusion(), kind=kLoop, calls=%fused_computation.29 | loop fusion | flops 3932160 | bytes 2097152 | tf_op jit(solution)/shard_map/neg | solution.py:40
  109.2 5.6 %collective-permute-start.15 = (bf16[512,256]{1,0:T(8,128)(2,1)S(1)}, bf16[512,256]{1,0:T(8,128)(2,1)S(1)}, u32[]{:S(2)}, u32[]{:S(2)}) collective-permute-start(bf16[512,256]{1,0:T(8,128)(2,1)S(1)} %collective-permute-done.14), channel_id=1, source_target_pairs={{0,120},{8,0},{16,8},{24,16},{32,24},{40,32},{48,40},{56,48},{64,5... | collective-permute-start | bytes 786440 | tf_op jit(solution)/shard_map/ppermute | solution.py:16
  116.2 1.7 constant_dynamic-update-slice_fusion.29
  118.0 1.7 constant_dynamic-update-slice_fusion.28
  123.3 0.8 constant_dynamic-update-slice_fusion.22
  124.1 0.8 constant_dynamic-update-slice_fusion.21
  125.6 0.8 constant_dynamic-update-slice_fusion.19
  126.4 0.8 constant_dynamic-update-slice_fusion.18
  127.9 0.8 constant_dynamic-update-slice_fusion.16
  130.2 1.7 constant_dynamic-update-slice_fusion.13
  131.8 0.8 constant_dynamic-update-slice_fusion.12
  134.8 0.8 constant_dynamic-update-slice_fusion.8
  136.3 0.8 constant_dynamic-update-slice_fusion.6
  138.6 0.7 constant_dynamic-update-slice_fusion.3
  139.3 6.7 %convert_element_type.67 = f32[4096,512]{1,0:T(8,128)} convert(bf16[4096,512]{1,0:T(8,128)(2,1)} %all-gather.4.cloned.1.call-done) | non-fusion elementwise | flops 2097152 | bytes 12582912 | tf_op jit(solution)/shard_map/convert_element_type | solution.py:82
  146.2 7.0 %while.16 = (s32[]{:T(128)}, f32[512,1024]{1,0:T(8,128)S(1)}, s32[]{:T(128)}, bf16[16,256,512]{2,1,0:T(8,128)(2,1)}, bf16[256,1024]{1,0:T(8,128)(2,1)}, /*index=...) while((s32[]{:T(128)}, f32[512,1024]{1,0:T(8,128)S(1)}, ...), condition=%wide.region_3.4_spmd, body=%wide.region_0.3_spmd.sunk | while | flops 1345323008 | bytes 24117560 | solution.py:103
  146.3 6.4 %conditional.2 = (f32[512,1024]{1,0:T(8,128)S(1)}) conditional(s32[]{:T(128)} %convert_element_type.104, f32[512,1024]{1,0:T(8,128)S(1)} %get-tuple-element.261, (s32[]{:T(128)}, bf16[16,256,512]{2,1,0:T(8,128)(2,1)}, bf16[256,1024]{1,0:T(8,128)(2,1)}, bf16[256,1024]{1,0:T(8,128)(2,1)}, s32[]{:T(128)}, /*index=5*/f32[4096,512]{1,0:T(8,128)}, ...), branch_computations={%region_1.1_spmd, %region_2.2_spmd} | conditional | flops 1345323008 | bytes 24117360 | solution.py:101
  146.3 2.1 fusion
  148.4 1.6 fusion.3
  150.0 1.6 convolution_add_fusion
  153.3 5.0 %fusion.11 = f32[512,512]{1,0:T(8,128)S(1)} fusion(f32[512,1024]{1,0:T(8,128)S(1)} %get-tuple-element.176, f32[512,512]{1,0:T(8,128)} %get-tuple-element.199, f32[512,512]{1,0:T(8,128)} %get-tuple-element.200), kind=kOutput, calls=%fused_computation.17 | convolution fusion | flops 1611661312 | bytes 5242880 | tf_op jit(solution)/shard_map/dot_general | solution.py:104
  158.4 5.0 %collective-permute-start = (bf16[256,512]{1,0:T(8,128)(2,1)S(1)}, bf16[256,512]{1,0:T(8,128)(2,1)S(1)}, u32[]{:S(2)}, u32[]{:S(2)}) collective-permute-start(bf16[256,512]{1,0:T(8,128)(2,1)S(1)} %slice.44), channel_id=1, source_target_pairs={{0,8},{8,16},{16,24},{24,32},{32,40},{40,48},{48,56},{56,64},{64,7... | collective-permute-start | bytes 786440 | tf_op jit(solution)/shard_map/ppermute | solution.py:24
  163.3 1.7 constant_dynamic-update-slice_fusion.2
  165.0 1.7 constant_dynamic-update-slice_fusion.1
  166.7 1.7 constant_dynamic-update-slice_fusion
  168.4 4.9 %convolution_convert_fusion = bf16[256,4096]{1,0:T(8,128)(2,1)} fusion(bf16[512,8192]{1,0:T(8,128)(2,1)} %constant_dynamic-update-slice_fusion, s32[]{:T(128)S(6)} %select_n.39, f32[512,512]{1,0:T(8,128)S(1)} %fusion.11, bf16[256,512]{1,0:T(8,128)(2,1)S(1)} %copy-done, bf16[256,512]{1,0:T(8,128)(2,1)S(1)} %collective-permute-done, ...), kind=kOutput, calls=%fused_computation.14 | convolution fusion | flops 1075838976 | bytes 7604228 | tf_op jit(solution)/shard_map/dot_general | solution.py:116
  173.3 125.4 %reduce-scatter.2.cloned.1.call-done = bf16[256,512]{1,0:T(8,128)(2,1)} async-done(((bf16[256,4096]{1,0:T(8,128)(2,1)}), bf16[256,512]{1,0:T(8,128)(2,1)}) %reduce-scatter.2.cloned.1.call-update) | async-done | bytes 262160 | tf_op jit(solution)/shard_map/reduce_scatter | solution.py:119
  (74 shorter events, 14.1 us)
Async XLA Ops:
  6.5 116.0 %copy-start.1 = (bf16[512,256]{1,0:T(8,128)(2,1)S(1)}, bf16[512,256]{1,0:T(8,128)(2,1)}, u32[]{:S(2)}) copy-start(bf16[512,256]{1,0:T(8,128)(2,1)} %param.15) | copy-start | bytes 786436
  6.5 132.8 %all-gather.4.cloned.1.call-start = ((), (), s32[]{:S(2)}) async-start(), calls=%async_computation.1 | async-start | bytes 4456448 | tf_op jit(solution)/shard_map/all_gather | solution.py:82
  8.4 137.6 %all-gather.6.cloned.1.call-start = ((), (), s32[]{:S(2)}) async-start(), calls=%async_computation.3 | async-start | bytes 4456448 | tf_op jit(solution)/shard_map/all_gather | solution.py:87
  10.2 288.5 %reduce-scatter.2.cloned.1.call-start = ((), (), s32[]{:S(2)}) async-start(), calls=%async_computation.2 | async-start | bytes 2359296 | tf_op jit(solution)/shard_map/reduce_scatter | solution.py:119
  10.3 13.2 %collective-permute-start.1 = (bf16[512,256]{1,0:T(8,128)(2,1)}, bf16[512,256]{1,0:T(8,128)(2,1)S(1)}, u32[]{:S(2)}, u32[]{:S(2)}) collective-permute-start(bf16[512,256]{1,0:T(8,128)(2,1)} %param.15), channel_id=1, source_target_pairs={{0,8},{8,16},{16,24},{24,32},{32,40},{40,48},{48,56},{56,64},{64,7... | collective-permute-start | bytes 786440 | tf_op jit(solution)/shard_map/ppermute | solution.py:14
  23.4 14.6 %collective-permute-start.2 = (bf16[512,256]{1,0:T(8,128)(2,1)S(1)}, bf16[512,256]{1,0:T(8,128)(2,1)S(1)}, u32[]{:S(2)}, u32[]{:S(2)}) collective-permute-start(bf16[512,256]{1,0:T(8,128)(2,1)S(1)} %collective-permute-done.1), channel_id=1, source_target_pairs={{0,8},{8,16},{16,24},{24,32},{32,40},{40,48},{48,56},{56,64},{64,7... | collective-permute-start | bytes 786440 | tf_op jit(solution)/shard_map/ppermute | solution.py:14
  23.4 14.6 %collective-permute-start.9 = (bf16[512,256]{1,0:T(8,128)(2,1)}, bf16[512,256]{1,0:T(8,128)(2,1)S(1)}, u32[]{:S(2)}, u32[]{:S(2)}) collective-permute-start(bf16[512,256]{1,0:T(8,128)(2,1)} %param.15), channel_id=1, source_target_pairs={{0,120},{8,0},{16,8},{24,16},{32,24},{40,32},{48,40},{56,48},{64,5... | collective-permute-start | bytes 786440 | tf_op jit(solution)/shard_map/ppermute | solution.py:16
  38.0 10.7 %collective-permute-start.3 = (bf16[512,256]{1,0:T(8,128)(2,1)S(1)}, bf16[512,256]{1,0:T(8,128)(2,1)S(1)}, u32[]{:S(2)}, u32[]{:S(2)}) collective-permute-start(bf16[512,256]{1,0:T(8,128)(2,1)S(1)} %collective-permute-done.2), channel_id=1, source_target_pairs={{0,8},{8,16},{16,24},{24,32},{32,40},{40,48},{48,56},{56,64},{64,7... | collective-permute-start | bytes 786440 | tf_op jit(solution)/shard_map/ppermute | solution.py:14
  38.0 14.1 %collective-permute-start.10 = (bf16[512,256]{1,0:T(8,128)(2,1)S(1)}, bf16[512,256]{1,0:T(8,128)(2,1)S(1)}, u32[]{:S(2)}, u32[]{:S(2)}) collective-permute-start(bf16[512,256]{1,0:T(8,128)(2,1)S(1)} %collective-permute-done.9), channel_id=1, source_target_pairs={{0,120},{8,0},{16,8},{24,16},{32,24},{40,32},{48,40},{56,48},{64,5... | collective-permute-start | bytes 786440 | tf_op jit(solution)/shard_map/ppermute | solution.py:16
  48.7 17.1 %collective-permute-start.4 = (bf16[512,256]{1,0:T(8,128)(2,1)S(1)}, bf16[512,256]{1,0:T(8,128)(2,1)S(1)}, u32[]{:S(2)}, u32[]{:S(2)}) collective-permute-start(bf16[512,256]{1,0:T(8,128)(2,1)S(1)} %collective-permute-done.3), channel_id=1, source_target_pairs={{0,8},{8,16},{16,24},{24,32},{32,40},{40,48},{48,56},{56,64},{64,7... | collective-permute-start | bytes 786440 | tf_op jit(solution)/shard_map/ppermute | solution.py:14
  52.1 15.8 %collective-permute-start.11 = (bf16[512,256]{1,0:T(8,128)(2,1)S(1)}, bf16[512,256]{1,0:T(8,128)(2,1)S(1)}, u32[]{:S(2)}, u32[]{:S(2)}) collective-permute-start(bf16[512,256]{1,0:T(8,128)(2,1)S(1)} %collective-permute-done.10), channel_id=1, source_target_pairs={{0,120},{8,0},{16,8},{24,16},{32,24},{40,32},{48,40},{56,48},{64,5... | collective-permute-start | bytes 786440 | tf_op jit(solution)/shard_map/ppermute | solution.py:16
  65.8 13.9 %collective-permute-start.5 = (bf16[512,256]{1,0:T(8,128)(2,1)S(1)}, bf16[512,256]{1,0:T(8,128)(2,1)S(1)}, u32[]{:S(2)}, u32[]{:S(2)}) collective-permute-start(bf16[512,256]{1,0:T(8,128)(2,1)S(1)} %collective-permute-done.4), channel_id=1, source_target_pairs={{0,8},{8,16},{16,24},{24,32},{32,40},{40,48},{48,56},{56,64},{64,7... | collective-permute-start | bytes 786440 | tf_op jit(solution)/shard_map/ppermute | solution.py:14
  67.9 11.9 %collective-permute-start.12 = (bf16[512,256]{1,0:T(8,128)(2,1)S(1)}, bf16[512,256]{1,0:T(8,128)(2,1)S(1)}, u32[]{:S(2)}, u32[]{:S(2)}) collective-permute-start(bf16[512,256]{1,0:T(8,128)(2,1)S(1)} %collective-permute-done.11), channel_id=1, source_target_pairs={{0,120},{8,0},{16,8},{24,16},{32,24},{40,32},{48,40},{56,48},{64,5... | collective-permute-start | bytes 786440 | tf_op jit(solution)/shard_map/ppermute | solution.py:16
  79.8 12.6 %copy-start.5 = (bf16[512,256]{1,0:T(8,128)(2,1)}, bf16[512,256]{1,0:T(8,128)(2,1)S(1)}, u32[]{:S(2)}) copy-start(bf16[512,256]{1,0:T(8,128)(2,1)S(1)} %collective-permute-done.5) | copy-start | bytes 786436
  79.8 10.5 %collective-permute-start.6 = (bf16[512,256]{1,0:T(8,128)(2,1)S(1)}, bf16[512,256]{1,0:T(8,128)(2,1)}, u32[]{:S(2)}, u32[]{:S(2)}) collective-permute-start(bf16[512,256]{1,0:T(8,128)(2,1)S(1)} %collective-permute-done.5), channel_id=1, source_target_pairs={{0,8},{8,16},{16,24},{24,32},{32,40},{40,48},{48,56},{56,64},{64,7... | collective-permute-start | bytes 786440 | tf_op jit(solution)/shard_map/ppermute | solution.py:14
  79.8 13.6 %collective-permute-start.13 = (bf16[512,256]{1,0:T(8,128)(2,1)S(1)}, bf16[512,256]{1,0:T(8,128)(2,1)S(1)}, u32[]{:S(2)}, u32[]{:S(2)}) collective-permute-start(bf16[512,256]{1,0:T(8,128)(2,1)S(1)} %collective-permute-done.12), channel_id=1, source_target_pairs={{0,120},{8,0},{16,8},{24,16},{32,24},{40,32},{48,40},{56,48},{64,5... | collective-permute-start | bytes 786440 | tf_op jit(solution)/shard_map/ppermute | solution.py:16
  90.3 13.1 %collective-permute-start.7 = (bf16[512,256]{1,0:T(8,128)(2,1)}, bf16[512,256]{1,0:T(8,128)(2,1)S(1)}, u32[]{:S(2)}, u32[]{:S(2)}) collective-permute-start(bf16[512,256]{1,0:T(8,128)(2,1)} %collective-permute-done.6), channel_id=1, source_target_pairs={{0,8},{8,16},{16,24},{24,32},{32,40},{40,48},{48,56},{56,64},{64,7... | collective-permute-start | bytes 786440 | tf_op jit(solution)/shard_map/ppermute | solution.py:14
  92.4 39.5 %copy-start.6 = (bf16[512,256]{1,0:T(8,128)(2,1)S(1)}, bf16[512,256]{1,0:T(8,128)(2,1)}, u32[]{:S(2)}) copy-start(bf16[512,256]{1,0:T(8,128)(2,1)} %copy-done.5) | copy-start | bytes 786436
  93.3 43.0 %copy-start.2 = (bf16[512,256]{1,0:T(8,128)(2,1)}, bf16[512,256]{1,0:T(8,128)(2,1)S(1)}, u32[]{:S(2)}) copy-start(bf16[512,256]{1,0:T(8,128)(2,1)S(1)} %collective-permute-done.13) | copy-start | bytes 786436
  93.3 15.9 %collective-permute-start.14 = (bf16[512,256]{1,0:T(8,128)(2,1)S(1)}, bf16[512,256]{1,0:T(8,128)(2,1)S(1)}, u32[]{:S(2)}, u32[]{:S(2)}) collective-permute-start(bf16[512,256]{1,0:T(8,128)(2,1)S(1)} %collective-permute-done.13), channel_id=1, source_target_pairs={{0,120},{8,0},{16,8},{24,16},{32,24},{40,32},{48,40},{56,48},{64,5... | collective-permute-start | bytes 786440 | tf_op jit(solution)/shard_map/ppermute | solution.py:16
  103.3 11.4 %collective-permute-start.8 = (bf16[512,256]{1,0:T(8,128)(2,1)S(1)}, bf16[512,256]{1,0:T(8,128)(2,1)S(1)}, u32[]{:S(2)}, u32[]{:S(2)}) collective-permute-start(bf16[512,256]{1,0:T(8,128)(2,1)S(1)} %collective-permute-done.7), channel_id=1, source_target_pairs={{0,8},{8,16},{16,24},{24,32},{32,40},{40,48},{48,56},{56,64},{64,7... | collective-permute-start | bytes 786440 | tf_op jit(solution)/shard_map/ppermute | solution.py:14
  109.2 27.9 %copy-start.3 = (bf16[512,256]{1,0:T(8,128)(2,1)}, bf16[512,256]{1,0:T(8,128)(2,1)S(1)}, u32[]{:S(2)}) copy-start(bf16[512,256]{1,0:T(8,128)(2,1)S(1)} %collective-permute-done.14) | copy-start | bytes 786436
  109.2 18.7 %collective-permute-start.15 = (bf16[512,256]{1,0:T(8,128)(2,1)S(1)}, bf16[512,256]{1,0:T(8,128)(2,1)S(1)}, u32[]{:S(2)}, u32[]{:S(2)}) collective-permute-start(bf16[512,256]{1,0:T(8,128)(2,1)S(1)} %collective-permute-done.14), channel_id=1, source_target_pairs={{0,120},{8,0},{16,8},{24,16},{32,24},{40,32},{48,40},{56,48},{64,5... | collective-permute-start | bytes 786440 | tf_op jit(solution)/shard_map/ppermute | solution.py:16
  127.9 10.0 %copy-start.4 = (bf16[512,256]{1,0:T(8,128)(2,1)}, bf16[512,256]{1,0:T(8,128)(2,1)S(1)}, u32[]{:S(2)}) copy-start(bf16[512,256]{1,0:T(8,128)(2,1)S(1)} %collective-permute-done.15) | copy-start | bytes 786436
  146.2 22.2 %copy-start = (bf16[256,512]{1,0:T(8,128)(2,1)S(1)}, bf16[256,512]{1,0:T(8,128)(2,1)}, u32[]{:S(2)}) copy-start(bf16[256,512]{1,0:T(8,128)(2,1)} %multiply_convert_fusion) | copy-start | bytes 786436
  146.2 22.2 %copy-start.7 = (f32[512]{0:T(512)S(1)}, f32[512]{0:T(512)}, u32[]{:S(2)}) copy-start(f32[512]{0:T(512)} %param.14) | copy-start | bytes 6148
  158.4 10.0 %collective-permute-start = (bf16[256,512]{1,0:T(8,128)(2,1)S(1)}, bf16[256,512]{1,0:T(8,128)(2,1)S(1)}, u32[]{:S(2)}, u32[]{:S(2)}) collective-permute-start(bf16[256,512]{1,0:T(8,128)(2,1)S(1)} %slice.44), channel_id=1, source_target_pairs={{0,8},{8,16},{16,24},{24,32},{32,40},{40,48},{48,56},{56,64},{64,7... | collective-permute-start | bytes 786440 | tf_op jit(solution)/shard_map/ppermute | solution.py:24
Sparse Core Ops, SparseCore 0:
  9.5 67.4 all-gather.3
  79.1 55.6 all-gather.5
  173.5 125.1 reduce-scatter.1
